TPU v7x, 256 devices: a whole 4x4x8 slice. The times are simulated.
256 devices in a mesh: dp: 8 (over z_lo, x), seq: 32 (over y, z_hi, core).
Axes of the slice: x: 4, y: 4, z: 8 (z_hi: 4, z_lo: 2; z = z_hi * 2 + z_lo), core: 2. Of those that a mesh axis runs over, the one named last changes fastest.
Arguments:
- queries: bfloat16 [8, 4096, 4096], P('dp', 'seq'), may hold values from -5 to 5
- rotated_key_rows: bfloat16 [8, 4096, 512], P('dp', 'seq'), may hold values from -5 to 5
- hidden_states: bfloat16 [8, 4096, 8192], P('dp', 'seq'), may hold values from -6 to 6
- block_order: int32 [64], replicated, may hold values from 0 to 63, each once
- first_weight: bfloat16 [8192, 512], replicated, may hold values from -0.0625 to 0.0625
- first_bias: float32 [512], replicated, may hold values from -3 to 3
- output_weight: bfloat16 [4, 512], replicated, may hold values from -0.25 to 0.25
- output_bias: float32 [4], replicated, may hold values from -1 to 1
Outputs:
- token_attention_mass: float32 [8, 4, 4096], P('dp', None, 'seq')
- loss_value: float32 [], replicated
- step_first: float32 [8192, 512], P('seq')
- output_weight_step: float32 [4, 512], replicated
- step_bias: float32 [512], replicated
- grad_bias: float32 [4], replicated
All inputs are finite; a program needn't handle non-finite values.
Results may differ from a plain program's by a relative error of at most 0.0023.
Values may be sent and summed in bfloat16 or wider, within the bound.
A program may use at most 64 MiB of HBM per device.

v0:
```python
import math
import jax
import jax.numpy as jnp
from jax import lax
from jax.sharding import PartitionSpec as P

D = 8192
KEY_VALUE_HEADS = 4
HEAD_SIZE = 128
RETAIN_HIDDEN = 512
BLK = 64
QUERY_GROUP_SIZE = 8


def key_places(block_order, offset, amount):
    row_ids = offset + lax.iota(jnp.int32, amount)
    block_ids = row_ids // BLK
    block_table = lax.iota(jnp.int32, block_order.shape[0])
    anchor = jnp.sum(
        jnp.where(block_ids[:, None] == block_table[None, :], block_order[None, :], 0), axis=1
    )
    return anchor * BLK + row_ids % BLK


def raw_scores(head_queries, mass_portion):
    head_keys = mass_portion.reshape(mass_portion.shape[0], KEY_VALUE_HEADS, HEAD_SIZE)
    return jnp.einsum(
        "tkgd,nkd->kgtn", head_queries, head_keys, preferred_element_type=jnp.float32
    ) * HEAD_SIZE ** (-0.5)


def blockwise(mass_portion, offset, update, carried):
    rows_here = mass_portion.shape[0]
    inner = math.gcd(rows_here, BLK)

    def visit_block(step_index, running):
        local_start = step_index * inner
        sub_rows = lax.dynamic_slice_in_dim(mass_portion, local_start, inner, 0)
        return update(running, sub_rows, offset + local_start)

    return lax.fori_loop(0, rows_here // inner, visit_block, carried)


def normalizer_step(running, mass_portion, key_start, head_queries, query_pos, block_order):
    highest, summed = running
    key_pos = key_places(block_order, key_start, mass_portion.shape[0])

    def normalizer_compute_step():
        scores = raw_scores(head_queries, mass_portion)
        visible = query_pos[:, None] >= key_pos[None, :]
        masked = jnp.where(visible, scores, -1e30)
        raised = jnp.maximum(highest, jnp.max(masked, axis=-1))
        exponents = jnp.where(visible, jnp.exp(masked - raised[..., None]), 0.0)
        return (raised, summed * jnp.exp(highest - raised) + jnp.sum(exponents, axis=-1))

    return lax.cond(
        jnp.min(key_pos) > jnp.max(query_pos), lambda: (highest, summed), normalizer_compute_step
    )


def mass_step(mass_portion, key_start, head_queries, query_pos, log_total, block_order):
    amount = mass_portion.shape[0]
    key_pos = key_places(block_order, key_start, amount)

    def mass_compute_step():
        scores = raw_scores(head_queries, mass_portion)
        visible = query_pos[:, None] >= key_pos[None, :]
        masked = jnp.where(visible, scores, -1e30)
        weights = jnp.where(visible, jnp.exp(masked - log_total[..., None]), 0.0)
        return jnp.sum(weights, axis=(1, 2)) / QUERY_GROUP_SIZE

    return lax.cond(
        jnp.min(key_pos) > jnp.max(query_pos),
        lambda: jnp.zeros((KEY_VALUE_HEADS, amount), jnp.float32),
        mass_compute_step,
    )


def normalized_scores(value_rows, square_sum, entries):
    return value_rows / jnp.sqrt(square_sum / entries + 1e-06)


def per_device(
    queries,
    rotated_key_rows,
    hidden_states,
    block_order,
    first_weight,
    first_bias,
    output_weight,
    output_bias,
):
    local_row_slice = queries.shape[1]
    total_length = local_row_slice * lax.axis_size("seq")
    head_queries = queries.reshape(local_row_slice, KEY_VALUE_HEADS, QUERY_GROUP_SIZE, HEAD_SIZE)
    local_key_rows = rotated_key_rows.reshape(local_row_slice, KEY_VALUE_HEADS * HEAD_SIZE)
    query_pos = key_places(block_order, lax.axis_index("seq") * local_row_slice, local_row_slice)
    start_state = (
        jnp.full((KEY_VALUE_HEADS, QUERY_GROUP_SIZE, local_row_slice), -1e30, jnp.float32),
        jnp.zeros((KEY_VALUE_HEADS, QUERY_GROUP_SIZE, local_row_slice), jnp.float32),
    )

    def norm_update(running, sub_rows, key_start):
        return normalizer_step(running, sub_rows, key_start, head_queries, query_pos, block_order)

    empty_mass = jnp.zeros((KEY_VALUE_HEADS, total_length), jnp.float32)
    keys_whole = lax.all_gather(local_key_rows, "seq", axis=0, tiled=True)
    highest, summed = blockwise(keys_whole, 0, norm_update, start_state)
    log_total = highest + jnp.log(summed)

    def add_kept(collected, sub_rows, key_start):
        term = mass_step(sub_rows, key_start, head_queries, query_pos, log_total, block_order)
        return lax.dynamic_update_slice_in_dim(collected, term, key_start, 1)

    column_mass = blockwise(keys_whole, 0, add_kept, empty_mass)
    key_attention_mass = lax.psum_scatter(column_mass, "seq", scatter_dimension=1, tiled=True)
    tokens_in = hidden_states.reshape(local_row_slice, hidden_states.shape[2])
    pre_act = jnp.dot(tokens_in, first_weight, preferred_element_type=jnp.float32) + first_bias
    hidden = jax.nn.silu(pre_act).astype(jnp.bfloat16)
    predicted_scores = (
        lax.dot_general(
            output_weight, hidden, (((1,), (1,)), ((), ())), preferred_element_type=jnp.float32
        )
        + output_bias[:, None]
    )
    score_residue = predicted_scores - jnp.log(1.0 + key_attention_mass)
    loss_part = 0.5 * jnp.sum(score_residue * score_residue) / total_length
    out_grad = score_residue / total_length
    bias_part = jnp.sum(out_grad, axis=1)
    second_part = jnp.dot(out_grad, hidden.astype(jnp.float32), precision=lax.Precision.HIGHEST)
    back_grad = jnp.dot(
        out_grad.T, output_weight.astype(jnp.float32), precision=lax.Precision.HIGHEST
    )
    gate_value = jax.nn.sigmoid(pre_act)
    slope_grad = back_grad * gate_value * (1.0 + pre_act * (1.0 - gate_value))
    first_bias_part = jnp.sum(slope_grad, axis=0)
    slope_half = slope_grad.astype(jnp.bfloat16)
    columns_all = lax.all_to_all(tokens_in, "seq", split_axis=1, concat_axis=0, tiled=True)
    slope_all = lax.all_gather(slope_half, "seq", axis=0, tiled=True)
    first_shard = lax.dot_general(
        columns_all, slope_all, (((0,), (0,)), ((), ())), preferred_element_type=jnp.float32
    )
    output_total, first_bias_total, bias_total, loss_total = lax.psum(
        (second_part, first_bias_part, bias_part, loss_part), ("dp", "seq")
    )
    first_grad = lax.psum(first_shard, "dp")
    first_square = lax.psum(jnp.sum(first_grad * first_grad), "seq")
    step_first = normalized_scores(first_grad, first_square, D * RETAIN_HIDDEN)
    output_weight_step = normalized_scores(
        output_total, jnp.sum(output_total * output_total), RETAIN_HIDDEN * KEY_VALUE_HEADS
    )
    step_bias = normalized_scores(
        first_bias_total, jnp.sum(first_bias_total * first_bias_total), RETAIN_HIDDEN
    )
    return (
        key_attention_mass.reshape(1, KEY_VALUE_HEADS, local_row_slice),
        loss_total,
        step_first,
        output_weight_step,
        step_bias,
        bias_total,
    )


def solution(mesh):
    in_specs = (
        P("dp", "seq", None),
        P("dp", "seq", None),
        P("dp", "seq", None),
        P(),
        P(),
        P(),
        P(),
        P(),
    )
    out_specs = (P("dp", None, "seq"), P(), P("seq", None), P(), P(), P())
    return jax.shard_map(
        per_device, mesh=mesh, in_specs=in_specs, out_specs=out_specs, check_vma=False
    )
```

profile of v0, /device:TPU:1, one launch (start us, length us, event | category | flops | bytes accessed | tf_op | source)
XLA Modules:
  0.0 925.9 jit_solution(2229353486682803280)
XLA Ops:
  11.0 64.1 %all-gather.6.cloned.1.call-done = bf16[1,4096,512]{2,1,0:T(8,128)(2,1)} async-done(((bf16[1,128,512]{2,1,0:T(8,128)(2,1)}), bf16[1,4096,512]{2,1,0:T(8,128)(2,1)}) %all-gather.6.cloned.1.call-update) | async-done | bytes 4194320 | tf_op jit(solution)/shard_map/all_gather | solution.py:107
  75.1 206.3 %while.32 = (s32[]{:T(128)}, f32[4,8,128]{2,1,0:T(8,128)S(1)}, f32[4,8,128]{2,1,0:T(8,128)S(1)}, s32[64]{0:T(128)S(1)}, s32[]{:T(128)}, /*index=5*/s32[128]{0:T(...) while((s32[]{:T(128)}, f32[4,8,128]{2,1,0:T(8,128)S(1)}, ...), condition=%wide.region_9.10_spmd, body=%wide.region_2.9_spmd.sunk | while | flops 68712320 | bytes 3713545 | solution.py:41
  79.5 1.7 conditional.4
  83.4 1.7 conditional.4
  87.3 1.7 conditional.4
  91.3 1.7 conditional.4
  108.4 1.7 conditional.4
  112.3 1.7 conditional.4
  118.5 1.7 conditional.4
  122.4 1.7 conditional.4
  128.5 1.7 conditional.4
  132.4 1.7 conditional.4
  138.6 1.7 conditional.4
  144.7 1.7 conditional.4
  153.0 1.7 conditional.4
  156.9 1.7 conditional.4
  160.9 1.7 conditional.4
  169.2 1.7 conditional.4
  173.1 1.7 conditional.4
  181.0 1.7 conditional.4
  184.9 1.7 conditional.4
  193.2 1.7 conditional.4
  199.3 1.7 conditional.4
  213.8 1.7 conditional.4
  217.7 1.7 conditional.4
  221.6 1.7 conditional.4
  225.6 1.7 conditional.4
  231.7 1.7 conditional.4
  235.6 1.7 conditional.4
  239.5 1.7 conditional.4
  249.6 1.7 conditional.4
  253.5 1.7 conditional.4
  257.4 1.7 conditional.4
  265.2 1.7 conditional.4
  269.1 1.7 conditional.4
  279.7 1.7 conditional.4
  281.5 212.6 %while.33 = (s32[]{:T(128)}, f32[4,4096]{1,0:T(4,128)S(1)}, s32[64]{0:T(128)S(1)}, s32[]{:T(128)}, s32[128]{0:T(128)S(1)}, /*index=5*/bf16[4096,512]{1,0:T(8,128...) while((s32[]{:T(128)}, f32[4,4096]{1,0:T(4,128)S(1)}, ...), condition=%wide.region_16.17_spmd, body=%wide.region_10.16_spmd.sunk | while | flops 68441992 | bytes 1416701 | solution.py:41
  494.1 2.0 copy.51
  496.2 4.8 multiply_convert_fusion
  501.0 164.5 %reduce-scatter.4.cloned.1.call-done = f32[128,4]{1,0:T(8,128)} async-done(((f32[4096,4]{1,0:T(8,128)}), f32[128,4]{1,0:T(8,128)}) %reduce-scatter.4.cloned.1.call-update) | async-done | bytes 2064
  668.3 2.5 copy.42
  670.8 63.7 %all_to_all.19 = bf16[128,32,256]{0,2,1:T(8,128)(2,1)S(1)} all-to-all(bf16[128,32,256]{0,2,1:T(8,128)(2,1)} %bitcast.50), channel_id=1, replica_groups=mesh['dp'=8,'seq'=32] {'seq'}, dimensions={1} | all-to-all | bytes 4194304 | tf_op jit(solution)/shard_map/all_to_all | solution.py:138
  734.5 2.9 copy.43
  737.4 19.9 %all-gather.4.cloned.1.call-done = bf16[4096,512]{1,0:T(8,128)(2,1)} async-done(((bf16[128,512]{1,0:T(8,128)(2,1)}), bf16[4096,512]{1,0:T(8,128)(2,1)}) %all-gather.4.cloned.1.call-update) | async-done | bytes 4194320 | tf_op jit(solution)/shard_map/all_gather | solution.py:139
  757.3 4.9 convolution_bitcast_fusion
  763.1 77.0 %all-reduce = (f32[]{:T(128)}, f32[4,512]{1,0:T(4,128)S(1)}, f32[512]{0:T(512)S(1)}, f32[4]{0:T(128)}) all-reduce(f32[]{:T(128)S(6)} %div.87, f32[4,512]{1,0:T(4,128)S(1)} %fusion.20, f32[512]{0:T(512)S(1)} %get-tuple-element.630, f32[4]{0:T(128)S(1)} %get-tuple-element.583), channel_id=1, replica_groups=mesh['dp'=8,'seq'=32] {'dp','seq'}, use_global_device_ids=true, to_apply=%region_19.20 | all-reduce | flops 2565 | bytes 20520 | tf_op jit(solution)/shard_map/psum | solution.py:143
  843.3 1.8 multiply_reduce_fusion
  845.7 70.9 %psum.44 = f32[]{:T(128)} all-reduce(f32[]{:T(128)} %multiply_reduce_fusion), channel_id=1, replica_groups=mesh['dp'=8,'seq'=32] {'seq'}, use_global_device_ids=true, to_apply=%region_22.23 | all-reduce | flops 1 | bytes 8 | tf_op jit(solution)/shard_map/psum | solution.py:147
  (1154 shorter events, 322.9 us)
Async XLA Ops:
  7.2 659.3 %copy-start = (bf16[4,512]{1,0:T(4,128)(2,1)S(1)}, bf16[4,512]{1,0:T(4,128)(2,1)}, u32[]{:S(2)}) copy-start(bf16[4,512]{1,0:T(4,128)(2,1)} %param.22) | copy-start | bytes 12292
  7.2 3.1 copy-start.4
  7.2 67.9 %all-gather.6.cloned.1.call-start = ((), (), s32[]{:S(2)}) async-start(), calls=%async_computation.4 | async-start | bytes 4325376 | tf_op jit(solution)/shard_map/all_gather | solution.py:107
  7.9 657.6 %reduce-scatter.4.cloned.1.call-start = ((), (), s32[]{:S(2)}) async-start(), calls=%async_computation.5 | async-start | bytes 2162688
  494.1 2.1 copy-start.1
  494.1 2.1 copy-start.2
  496.1 170.4 %copy-start.5 = (f32[4]{0:T(128)S(1)}, f32[4]{0:T(128)}, u32[]{:S(2)}) copy-start(f32[4]{0:T(128)} %param.23) | copy-start | bytes 52
  496.1 261.2 %all-gather.4.cloned.1.call-start = ((), (), s32[]{:S(2)}) async-start(), calls=%async_computation.2 | async-start | bytes 4325376 | tf_op jit(solution)/shard_map/all_gather | solution.py:139
  666.4 68.1 %copy-start.3 = (f32[4,128]{1,0:T(4,128)}, f32[4,128]{1,0:T(4,128)S(1)}, u32[]{:S(2)}) copy-start(f32[4,128]{1,0:T(4,128)S(1)} %copy.52) | copy-start | bytes 6148
  668.2 175.1 %all-reduce.3.cloned.1.call-start = ((), (), s32[]{:S(2)}) async-start(), calls=%async_computation.3 | async-start | bytes 1048576 | tf_op jit(solution)/shard_map/psum | solution.py:146
Sparse Core Ops, SparseCore 0:
  10.6 64.5 all-gather.5
  496.2 169.2 reduce-scatter.3
  668.7 88.6 all-gather.3
  762.4 72.5 all-reduce.2
where the time goes:
time: 935 us; the launch traced here: 926 us
  waiting for transfers between devices  249 us (27%)
  blocking collectives  212 us (23%)
  loops' own time  175 us (19%)
  other arithmetic  128 us (14%)
  local copies, waits for them, and re-layouts  92.1 us (10%)
  matrix products  52.9 us (6%)
  between operations  16.7 us (2%)
    another operation x2, loops' own time, blockwise(): return lax.fori_loop(0, rows_here // inner, visit_block, carried)  171 us
    unnamed x5, waiting for transfers between devices  165 us
    psum x1, blocking collectives, per_device(): lax.psum((second_part, first_bias_part, bias_part, loss_part), ('dp', 'se...  77 us
    psum x1, blocking collectives, per_device(): first_square = lax.psum(jnp.sum(first_grad * first_grad), 'seq')  70.9 us
    dynamic_slice x76, local copies, waits for them, and re-layouts, visit_block(): sub_rows = lax.dynamic_slice_in_dim(mass_portion, local_start, inner, 0)  64.7 us
    all_gather x1, waiting for transfers between devices, per_device(): keys_whole = lax.all_gather(local_key_rows, 'seq', axis=0, tiled=True)  64.1 us
    all_to_all x1, blocking collectives, per_device(): lax.all_to_all(tokens_in, 'seq', split_axis=1, concat_axis=0, tiled=True)  63.7 us
    reduce_min x64, other arithmetic, normalizer_step(): jnp.min(key_pos) > jnp.max(query_pos)  41.8 us
  transfers between devices with their start and end apart: 4, of which 3 were waited for; matrix products, arithmetic and copies ran while one was open for 2% of the time, Pallas kernels for 0%

commit v1 on v0

--- a/solution.py
+++ b/solution.py
@@ -141,7 +141,7 @@
         columns_all, slope_all, (((0,), (0,)), ((), ())), preferred_element_type=jnp.float32
     )
     output_total, first_bias_total, bias_total, loss_total = lax.psum(
-        (second_part, first_bias_part, bias_part, loss_part), ("dp", "seq")
+        lax.psum((second_part, first_bias_part, bias_part, loss_part), "seq"), "dp"
     )
     first_grad = lax.psum(first_shard, "dp")
     first_square = lax.psum(jnp.sum(first_grad * first_grad), "seq")

time: 935 us -> 1030 us (1.10)
  waiting for transfers between devices: 249 us -> 321 us
  blocking collectives: 212 us -> 227 us
    psum x1, waiting for transfers between devices: 0.01 us -> 71.9 us  [per_device(): first_grad = lax.psum(first_shard, 'dp')]
    psum x2, blocking collectives: 148 us -> 163 us  [the longest x1 138 us: per_device(): lax.psum((second_part, first_bias_part, bias_part, loss_part), 'seq')]
  transfers between devices with their start and end apart: 4 -> 4, of which waited for: 3 -> 4; matrix products, arithmetic and copies ran while one was open for 2% -> 1% of each run, Pallas kernels for 0% -> 0%
where the time goes in v1:
time: 1030 us; the launch traced here: 1010 us
  waiting for transfers between devices  321 us (31%)
  blocking collectives  227 us (22%)
  loops' own time  175 us (17%)
  other arithmetic  128 us (12%)
  local copies, waits for them, and re-layouts  92.1 us (9%)
  matrix products  52.9 us (5%)
  between operations  16.6 us (2%)
    another operation x2, loops' own time, blockwise(): return lax.fori_loop(0, rows_here // inner, visit_block, carried)  171 us
    unnamed x5, waiting for transfers between devices  165 us
    psum x1, blocking collectives, per_device(): lax.psum((second_part, first_bias_part, bias_part, loss_part), 'seq')  138 us
    psum x1, waiting for transfers between devices, per_device(): first_grad = lax.psum(first_shard, 'dp')  71.9 us
    dynamic_slice x76, local copies, waits for them, and re-layouts, visit_block(): sub_rows = lax.dynamic_slice_in_dim(mass_portion, local_start, inner, 0)  64.7 us
    all_gather x1, waiting for transfers between devices, per_device(): keys_whole = lax.all_gather(local_key_rows, 'seq', axis=0, tiled=True)  64.1 us
    all_to_all x1, blocking collectives, per_device(): lax.all_to_all(tokens_in, 'seq', split_axis=1, concat_axis=0, tiled=True)  63.7 us
    reduce_min x64, other arithmetic, normalizer_step(): jnp.min(key_pos) > jnp.max(query_pos)  41.8 us
  transfers between devices with their start and end apart: 4, of which 4 were waited for; matrix products, arithmetic and copies ran while one was open for 1% of the time, Pallas kernels for 0%

profile of v1, /device:TPU:1, one launch (start us, length us, event | category | flops | bytes accessed | tf_op | source)
XLA Modules:
  0.0 1012.8 jit_solution(16904194593461795754)
XLA Ops:
  11.0 64.1 %all-gather.6.cloned.1.call-done = bf16[1,4096,512]{2,1,0:T(8,128)(2,1)} async-done(((bf16[1,128,512]{2,1,0:T(8,128)(2,1)}), bf16[1,4096,512]{2,1,0:T(8,128)(2,1)}) %all-gather.6.cloned.1.call-update) | async-done | bytes 4194320 | tf_op jit(solution)/shard_map/all_gather | solution.py:107
  75.1 206.3 %while.32 = (s32[]{:T(128)}, f32[4,8,128]{2,1,0:T(8,128)S(1)}, f32[4,8,128]{2,1,0:T(8,128)S(1)}, s32[64]{0:T(128)S(1)}, s32[]{:T(128)}, /*index=5*/s32[128]{0:T(...) while((s32[]{:T(128)}, f32[4,8,128]{2,1,0:T(8,128)S(1)}, ...), condition=%wide.region_9.10_spmd, body=%wide.region_2.9_spmd.sunk | while | flops 68712320 | bytes 3713545 | solution.py:41
  79.5 1.7 conditional.4
  83.4 1.7 conditional.4
  87.3 1.7 conditional.4
  91.3 1.7 conditional.4
  108.4 1.7 conditional.4
  112.3 1.7 conditional.4
  118.5 1.7 conditional.4
  122.4 1.7 conditional.4
  128.5 1.7 conditional.4
  132.4 1.7 conditional.4
  138.6 1.7 conditional.4
  144.7 1.7 conditional.4
  153.0 1.7 conditional.4
  156.9 1.7 conditional.4
  169.2 1.7 conditional.4
  173.1 1.7 conditional.4
  181.0 1.7 conditional.4
  184.9 1.7 conditional.4
  193.2 1.7 conditional.4
  199.3 1.7 conditional.4
  213.8 1.7 conditional.4
  217.7 1.7 conditional.4
  221.6 1.7 conditional.4
  225.6 1.7 conditional.4
  231.7 1.7 conditional.4
  235.6 1.7 conditional.4
  239.5 1.7 conditional.4
  249.6 1.7 conditional.4
  253.5 1.7 conditional.4
  257.4 1.7 conditional.4
  265.2 1.7 conditional.4
  269.1 1.7 conditional.4
  279.7 1.7 conditional.4
  281.5 212.6 %while.33 = (s32[]{:T(128)}, f32[4,4096]{1,0:T(4,128)S(1)}, s32[64]{0:T(128)S(1)}, s32[]{:T(128)}, s32[128]{0:T(128)S(1)}, /*index=5*/bf16[4096,512]{1,0:T(8,128...) while((s32[]{:T(128)}, f32[4,4096]{1,0:T(4,128)S(1)}, ...), condition=%wide.region_16.17_spmd, body=%wide.region_10.16_spmd.sunk | while | flops 68441992 | bytes 1416701 | solution.py:41
  494.1 2.0 copy.51
  496.2 4.8 multiply_convert_fusion
  501.0 164.5 %reduce-scatter.4.cloned.1.call-done = f32[128,4]{1,0:T(8,128)} async-done(((f32[4096,4]{1,0:T(8,128)}), f32[128,4]{1,0:T(8,128)}) %reduce-scatter.4.cloned.1.call-update) | async-done | bytes 2064
  668.3 2.5 copy.42
  670.8 63.7 %all_to_all.19 = bf16[128,32,256]{0,2,1:T(8,128)(2,1)S(1)} all-to-all(bf16[128,32,256]{0,2,1:T(8,128)(2,1)} %bitcast.50), channel_id=1, replica_groups=mesh['dp'=8,'seq'=32] {'seq'}, dimensions={1} | all-to-all | bytes 4194304 | tf_op jit(solution)/shard_map/all_to_all | solution.py:138
  734.5 2.9 copy.43
  737.4 19.9 %all-gather.4.cloned.1.call-done = bf16[4096,512]{1,0:T(8,128)(2,1)} async-done(((bf16[128,512]{1,0:T(8,128)(2,1)}), bf16[4096,512]{1,0:T(8,128)(2,1)}) %all-gather.4.cloned.1.call-update) | async-done | bytes 4194320 | tf_op jit(solution)/shard_map/all_gather | solution.py:139
  757.3 4.9 convolution_bitcast_fusion
  763.1 71.9 %all-reduce.4.cloned.1.call-done = f32[256,512]{0,1:T(8,128)} async-done(((f32[256,512]{0,1:T(8,128)}), f32[256,512]{0,1:T(8,128)}) %all-reduce.4.cloned.1.call-update) | async-done | bytes 524304 | tf_op jit(solution)/shard_map/psum | solution.py:146
  835.0 1.8 multiply_reduce_fusion
  836.8 137.7 %all-reduce = (f32[]{:T(128)}, f32[]{:T(128)}, f32[4,512]{1,0:T(4,128)S(1)}, f32[512]{0:T(512)S(1)}, f32[4]{0:T(128)S(1)}) all-reduce(f32[]{:T(128)S(6)} %div.87, f32[]{:T(128)} %multiply_reduce_fusion, f32[4,512]{1,0:T(4,128)S(1)} %fusion.20, f32[512]{0:T(512)S(1)} %get-tuple-element.634, ...), channel_id=1, replica_groups=mesh['dp'=8,'seq'=32] {'seq'}, use_global_device_ids=true, to_apply=%region_19.20 | all-reduce | flops 2566 | bytes 20528 | tf_op jit(solution)/shard_map/psum | solution.py:144
  977.3 25.2 %all-reduce.1 = (f32[]{:T(128)}, f32[4,512]{1,0:T(4,128)S(1)}, f32[512]{0:T(512)S(1)}, f32[4]{0:T(128)}) all-reduce(f32[]{:T(128)} %get-tuple-element.617, f32[4,512]{1,0:T(4,128)S(1)} %get-tuple-element.619, f32[512]{0:T(512)S(1)} %get-tuple-element.620, f32[4]{0:T(128)S(1)} %get-tuple-element.621), channel_id=1, replica_groups=mesh['dp'=8,'seq'=32] {'dp'}, use_global_device_ids=true, to_apply=%region_20.21 | all-reduce | flops 2565 | bytes 20520 | tf_op jit(solution)/shard_map/psum | solution.py:143
  (1154 shorter events, 324.6 us)
Async XLA Ops:
  7.2 659.3 %copy-start = (bf16[4,512]{1,0:T(4,128)(2,1)S(1)}, bf16[4,512]{1,0:T(4,128)(2,1)}, u32[]{:S(2)}) copy-start(bf16[4,512]{1,0:T(4,128)(2,1)} %param.22) | copy-start | bytes 12292
  7.2 3.1 copy-start.4
  7.2 67.9 %all-gather.6.cloned.1.call-start = ((), (), s32[]{:S(2)}) async-start(), calls=%async_computation.4 | async-start | bytes 4325376 | tf_op jit(solution)/shard_map/all_gather | solution.py:107
  7.9 657.6 %reduce-scatter.4.cloned.1.call-start = ((), (), s32[]{:S(2)}) async-start(), calls=%async_computation.5 | async-start | bytes 2162688
  494.1 2.1 copy-start.1
  494.1 2.1 copy-start.2
  496.1 170.4 %copy-start.5 = (f32[4]{0:T(128)S(1)}, f32[4]{0:T(128)}, u32[]{:S(2)}) copy-start(f32[4]{0:T(128)} %param.23) | copy-start | bytes 52
  496.1 261.2 %all-gather.4.cloned.1.call-start = ((), (), s32[]{:S(2)}) async-start(), calls=%async_computation.2 | async-start | bytes 4325376 | tf_op jit(solution)/shard_map/all_gather | solution.py:139
  666.4 68.1 %copy-start.3 = (f32[4,128]{1,0:T(4,128)}, f32[4,128]{1,0:T(4,128)S(1)}, u32[]{:S(2)}) copy-start(f32[4,128]{1,0:T(4,128)S(1)} %copy.52) | copy-start | bytes 6148
  668.2 166.8 %all-reduce.4.cloned.1.call-start = ((), (), s32[]{:S(2)}) async-start(), calls=%async_computation.3 | async-start | bytes 1048576 | tf_op jit(solution)/shard_map/psum | solution.py:146
Sparse Core Ops, SparseCore 0:
  10.6 64.5 all-gather.5
  496.2 169.2 reduce-scatter.3
  668.7 88.6 all-gather.3
  762.4 72.5 all-reduce.3
